TPU v7x, 256 devices: a whole 4x4x8 slice. The times are simulated.
256 devices in a mesh: dp: 8 (over x, core), ctx: 32 (over y, z).
Axes of the slice: x: 4, y: 4, z: 8, core: 2. Of those that a mesh axis runs over, the one named last changes fastest.
Arguments:
- features: bfloat16 [8, 4096, 6144], P('dp', 'ctx'), may hold values from -6 to 6
- upstream: bfloat16 [8, 4096, 2048], P('dp', 'ctx'), may hold values from -6 to 6
- lengths: int32 [8, 8], P('dp'), may hold values from 1 to 2048, 4096 in all within a row
- conv_taps: float32 [3, 6144], replicated, may hold values from -3 to 3
- residues: float32 [16, 2048], P(None, 'ctx'), may hold values from -0.12 to 0.12
- log_rate: float32 [16, 2048], P(None, 'ctx'), may hold values from -13.2 to -3.5
- skip_gain: float32 [2048], P('ctx'), may hold values from -4 to 4
Outputs:
- grad_features: bfloat16 [8, 4096, 6144], P('dp', 'ctx')
- grad_taps: float32 [3, 6144], replicated
- grad_residues: float32 [16, 2048], P(None, 'ctx')
- grad_skip: float32 [2048], P('ctx')
All inputs are finite; a program needn't handle non-finite values.
Results may differ from a plain program's by a relative error of at most 0.0095.
Values may be sent and summed in bfloat16 or wider, within the bound.
A program may use at most 192 MiB of HBM per device.

v0:
```python
import math
import jax
import jax.numpy as jnp
from jax import lax
from jax.sharding import PartitionSpec as P

BLOCK_ROWS = 128


def from_behind(block, axis, distance):
    devices = range(lax.axis_size(axis))
    route = [(i - distance, i) for i in devices if i - distance in devices]
    return lax.ppermute(block, axis, route)


def segment_of(positions, bounds):
    return jnp.sum((positions[:, None] >= bounds[None, :]).astype(jnp.int32), axis=1)


def segment_masks(positions, bounds, window_len):
    seg_ids = segment_of(positions, bounds)
    keep_one = ((positions >= 1) & (segment_of(positions - 1, bounds) == seg_ids)).astype(
        jnp.float32
    )
    keep_two = ((positions >= 2) & (segment_of(positions - 2, bounds) == seg_ids)).astype(
        jnp.float32
    )
    next_one = (
        (positions + 1 < window_len) & (segment_of(positions + 1, bounds) == seg_ids)
    ).astype(jnp.float32)
    next_two = (
        (positions + 2 < window_len) & (segment_of(positions + 2, bounds) == seg_ids)
    ).astype(jnp.float32)
    return (seg_ids, keep_one, keep_two, next_one, next_two)


def causal_taps(current, before, tap_rows, keep_one, keep_two):
    extended = jnp.concatenate([before, current], axis=0)
    return (
        tap_rows[0] * current
        + tap_rows[1] * (keep_one[:, None] * extended[1:-1])
        + tap_rows[2] * (keep_two[:, None] * extended[:-2])
    )


def transposed_taps(current, after, tap_rows, next_one, next_two):
    extended = jnp.concatenate([current, after], axis=0)
    return (
        tap_rows[0] * current
        + tap_rows[1] * (next_one[:, None] * extended[1:-1])
        + tap_rows[2] * (next_two[:, None] * extended[2:])
    )


def tap_terms(gradient, current, before, keep_one, keep_two):
    extended = jnp.concatenate([before, current], axis=0)
    first = jnp.sum(gradient * current, axis=0)
    second = jnp.sum(gradient * (keep_one[:, None] * extended[1:-1]), axis=0)
    third = jnp.sum(gradient * (keep_two[:, None] * extended[:-2]), axis=0)
    return jnp.stack([first, second, third])


def combine_states(earlier, later):
    return (earlier[0] * later[0], later[0] * earlier[1] + later[1])


def modal_sweep(source, segment_ids, decay_rate, coeff, other):
    length, chan_count = source.shape
    pole_count = decay_rate.shape[0]
    blocks = length // BLOCK_ROWS
    per_step = 4
    groups = blocks // per_step
    offsets = jnp.arange(BLOCK_ROWS, dtype=jnp.float32)
    rising = jnp.exp(decay_rate[None] * offsets[:, None, None])
    falling = jnp.exp(-decay_rate[None] * offsets[:, None, None])
    causal = offsets[:, None] >= offsets[None, :]

    def group_fn(inputs):
        src_blk, seg_blk, other_blk = inputs
        joined_mask = ((seg_blk[:, :, None] == seg_blk[:, None, :]) & causal[None]).astype(
            source.dtype
        )
        lifted = (src_blk[:, :, None, :] * rising[None]).reshape(
            per_step, BLOCK_ROWS, pole_count * chan_count
        )
        inner_state = jnp.einsum(
            "pij,pjk->pik", joined_mask, lifted, precision=lax.Precision.HIGHEST
        )
        inner_state = (
            inner_state.reshape(per_step, BLOCK_ROWS, pole_count, chan_count) * falling[None]
        )
        block_out = jnp.einsum("pimc,mc->pic", inner_state, coeff, precision=lax.Precision.HIGHEST)
        last_row = inner_state[:, -1]
        start_same = (seg_blk == seg_blk[:, :1]).astype(source.dtype)
        partial_sum = jnp.einsum(
            "pic,pimc->mc", other_blk, inner_state, precision=lax.Precision.HIGHEST
        )
        weights = jnp.einsum(
            "pic,imc->pmc",
            other_blk * start_same[:, :, None],
            falling,
            precision=lax.Precision.HIGHEST,
        )
        return (block_out, last_row, partial_sum, weights)

    src_groups = source.reshape(groups, per_step, BLOCK_ROWS, chan_count)
    seg_groups = segment_ids.reshape(groups, per_step, BLOCK_ROWS)
    other_groups = other.reshape(groups, per_step, BLOCK_ROWS, chan_count)
    block_out, last_row, partial_sum, weights = lax.map(
        group_fn, (src_groups, seg_groups, other_groups)
    )
    block_out = block_out.reshape(blocks, BLOCK_ROWS, chan_count)
    last_row = last_row.reshape(blocks, pole_count, chan_count)
    weights = weights.reshape(blocks, pole_count, chan_count)
    seg_rows = segment_ids.reshape(blocks, BLOCK_ROWS)
    starts = seg_rows[:, 0]
    finals = seg_rows[:, -1]
    joined = (starts[1:] == finals[:-1]).astype(source.dtype)
    through = (starts[:-1] == finals[:-1]).astype(source.dtype)
    one_step = jnp.exp(-decay_rate)
    block_decay = jnp.exp(-decay_rate * BLOCK_ROWS)
    factors = (joined * through)[:, None, None] * block_decay[None]
    inputs_in = joined[:, None, None] * one_step[None] * last_row[:-1]
    unused, states = lax.associative_scan(combine_states, (factors, inputs_in))
    carried = jnp.concatenate(
        [jnp.zeros((1, pole_count, chan_count), source.dtype), states], axis=0
    )
    start_rows = (seg_rows == starts[:, None]).astype(source.dtype)
    carry_out = (
        jnp.einsum("kmc,imc->kic", carried * coeff[None], falling, precision=lax.Precision.HIGHEST)
        * start_rows[:, :, None]
    )
    result = (block_out + carry_out).reshape(length, chan_count)
    grad_part = jnp.sum(partial_sum, axis=0) + jnp.einsum(
        "kmc,kmc->mc", weights, carried, precision=lax.Precision.HIGHEST
    )
    return (result, grad_part)


def per_device(features, upstream, lengths, conv_taps, residues, log_rate, skip_gain):
    feats = features[0]
    upf = upstream[0].astype(jnp.float32)
    tok_rows = feats.shape[0]
    channels = upstream.shape[2]
    ctx_count = lax.axis_size("ctx")
    shard_index = lax.axis_index("ctx")
    per_shard = channels // ctx_count
    window_len = tok_rows * ctx_count
    grad_scale = 1.0 / math.sqrt(window_len * lax.axis_size("dp"))
    bounds = jnp.cumsum(lengths[0])[:-1]
    local_pos = shard_index * tok_rows + jnp.arange(tok_rows, dtype=jnp.int32)
    seg_local, keep_one, keep_two, next_one, next_two = segment_masks(local_pos, bounds, window_len)
    whole_pos = jnp.arange(window_len, dtype=jnp.int32)
    seg_all, wkeep_one, wkeep_two, wnext_one, wnext_two = segment_masks(
        whole_pos, bounds, window_len
    )
    decay_rate = jnp.exp(log_rate)
    zero_rows = jnp.zeros((2, per_shard), jnp.float32)
    edge_rows = feats[-2:, :channels]
    before = from_behind(edge_rows, "ctx", 1).astype(jnp.float32)
    src_seq = feats[:, :channels].astype(jnp.float32)
    query_seq = causal_taps(src_seq, before, conv_taps[:, :channels], keep_one, keep_two)
    outgoing = feats[:, channels:].reshape(tok_rows, 2, channels)
    grad_out = (upf * query_seq).astype(jnp.bfloat16)[:, None, :]
    arrived = lax.all_to_all(outgoing, "ctx", split_axis=2, concat_axis=0, tiled=True)
    arrived_grad = lax.all_to_all(grad_out, "ctx", split_axis=2, concat_axis=0, tiled=True)
    tap_cols = lax.dynamic_slice(
        conv_taps.reshape(3, 3, channels), (0, 1, shard_index * per_shard), (3, 2, per_shard)
    )
    key_src = arrived[:, 0].astype(jnp.float32)
    val_src = arrived[:, 1].astype(jnp.float32)
    key_ch = causal_taps(key_src, zero_rows, tap_cols[:, 0], wkeep_one, wkeep_two)
    val_ch = causal_taps(val_src, zero_rows, tap_cols[:, 1], wkeep_one, wkeep_two)
    mixed_ch = (key_ch * val_ch).astype(jnp.bfloat16)
    mixedf = mixed_ch.astype(jnp.float32)
    conv_out, unused = modal_sweep(mixedf, seg_all, decay_rate, residues, jnp.zeros_like(mixedf))
    output_ch = (conv_out + skip_gain * mixedf).astype(jnp.bfloat16)
    gradf = arrived_grad[:, 0].astype(jnp.float32)
    adjoint, grad_resid = modal_sweep(
        gradf[::-1], seg_all[::-1], decay_rate, residues, mixedf[::-1]
    )
    grad_mixed = (adjoint[::-1] + skip_gain * gradf).astype(jnp.bfloat16)
    skip_part = jnp.sum(mixedf * gradf, axis=0)
    dmixf = grad_mixed.astype(jnp.float32)
    grad_key = dmixf * val_ch
    grad_val = dmixf * key_ch
    key_back = transposed_taps(grad_key, zero_rows, tap_cols[:, 0], wnext_one, wnext_two)
    val_back = transposed_taps(grad_val, zero_rows, tap_cols[:, 1], wnext_one, wnext_two)
    second = jnp.stack([key_back, val_back], axis=1).astype(jnp.bfloat16)
    kv_taps = jnp.stack(
        [
            tap_terms(grad_key, key_src, zero_rows, wkeep_one, wkeep_two),
            tap_terms(grad_val, val_src, zero_rows, wkeep_one, wkeep_two),
        ],
        axis=1,
    )
    first = output_ch[:, None, :]
    first_back = lax.all_to_all(first, "ctx", split_axis=0, concat_axis=2, tiled=True)
    second_back = lax.all_to_all(second, "ctx", split_axis=0, concat_axis=2, tiled=True)
    grad_query = upf * first_back[:, 0].astype(jnp.float32)
    rows_next = from_behind(grad_query[:2], "ctx", -1)
    grad_query_feats = transposed_taps(
        grad_query, rows_next, conv_taps[:, :channels], next_one, next_two
    ).astype(jnp.bfloat16)
    grad_feats = jnp.concatenate(
        [grad_query_feats, second_back.reshape(tok_rows, 2 * channels)], axis=1
    )
    placed = (
        jnp.zeros((3, 3, channels), jnp.float32)
        .at[:, 0, :]
        .set(tap_terms(grad_query, src_seq, before, keep_one, keep_two))
    )
    placed = lax.dynamic_update_slice(placed, kv_taps, (0, 1, shard_index * per_shard))
    tap_sum = placed.reshape(3, 3 * channels)
    grad_taps = lax.psum(tap_sum, ("dp", "ctx")) * grad_scale
    resid_sum, skip_sum = lax.psum((grad_resid, skip_part), "dp")
    return (grad_feats[None], grad_taps, resid_sum * grad_scale, skip_sum * grad_scale)


def solution(mesh):
    return jax.shard_map(
        per_device,
        mesh=mesh,
        in_specs=(
            P("dp", "ctx", None),
            P("dp", "ctx", None),
            P("dp", None),
            P(),
            P(None, "ctx"),
            P(None, "ctx"),
            P("ctx"),
        ),
        out_specs=(P("dp", "ctx", None), P(), P(None, "ctx"), P("ctx")),
        check_vma=False,
    )
```

profile of v0, /device:TPU:1, one launch (start us, length us, event | category | flops | bytes accessed | tf_op | source)
XLA Modules:
  0.0 609.8 jit_solution(1691059669882293001)
XLA Ops:
  7.2 1.9 copy.214
  9.1 1.2 slice.487
  10.4 5.2 collective-permute-start.1
  16.6 1.3 copy.213
  17.9 7.7 %collective-permute-done.1 = bf16[2,2048]{0,1:T(8,128)(2,1)} collective-permute-done((bf16[2,2048]{0,1:T(8,128)(2,1)}, bf16[2,2048]{0,1:T(8,128)(2,1)}, u32[]{:S(2)}, u32[]{:S(2)}) %collective-permute-start.1) | collective-permute-done | bytes 8224 | tf_op jit(solution)/shard_map/ppermute | solution.py:13
  26.7 1.9 fusion.46
  28.8 8.9 %copy.348 = bf16[128,1,2048]{0,1,2:T(2,128)(2,1)} copy(bf16[128,1,2048]{0,2,1:T(8,128)(2,1)S(1)} %fusion.46) | data formatting | bytes 1048576 | tf_op jit(solution)/shard_map/broadcast_in_dim | solution.py:164
  38.2 12.5 %reduce.26 = bf16[2048,128]{1,0:T(8,128)(2,1)S(1)} reduce(bf16[2048,1,128]{2,1,0:T(2,128)(2,1)} %bitcast.298, bf16[]{:T(256)} %broadcast.332), dimensions={1}, to_apply=%bitcast.221.reduce_sub_computation | reduce | bytes 1048578
  51.7 13.2 %all-to-all-start.2 = ((bf16[32,2,4096]{2,1,0:T(2,128)(2,1)}), bf16[32,2,4096]{2,1,0:T(2,128)(2,1)S(1)}, u32[]{:S(2)}, u32[]{:S(2)}) async-start(bf16[32,2,4096]{2,1,0:T(2,128)(2,1)} %reshape.467), calls=%async_computation.2 | async-start | bytes 1048576 | tf_op jit(solution)/shard_map/all_to_all | solution.py:166
  65.0 9.5 %copy.215 = bf16[128,2,2048]{0,1,2:T(2,128)(2,1)} copy(bf16[128,2,2048]{0,2,1:T(8,128)(2,1)S(1)} %bitcast.297) | data formatting | bytes 2097152 | tf_op jit(solution)/shard_map/reshape | solution.py:163
  76.2 1.5 all-to-all-done.2
  77.7 8.6 %all-to-all-start = ((bf16[128,2,2048]{0,1,2:T(2,128)(2,1)}), bf16[128,2,2048]{0,1,2:T(2,128)(2,1)S(1)}, u32[]{:S(2)}, u32[]{:S(2)}) async-start(bf16[128,2,2048]{0,1,2:T(2,128)(2,1)} %copy.215), calls=%async_computation | async-start | bytes 2097152 | tf_op jit(solution)/shard_map/all_to_all | solution.py:165
  91.3 1.6 copy.346
  92.9 13.4 %rev.13 = f32[4096,64]{0,1:T(8,128)S(1)} reverse(f32[4096,64]{0,1:T(8,128)} %bitcast.302), dimensions={0} | reverse | bytes 2097152 | tf_op jit(solution)/shard_map/rev | solution.py:180
  106.4 1.7 reshape.428
  108.0 2.9 all-to-all-done
  112.3 3.6 multiply_reduce_fusion.2
  115.9 2.6 rev.14
  118.4 1.8 reshape.422
  120.2 1.7 reshape.429
  122.3 90.9 %while.32 = (s32[]{:T(128)}, f32[8,4,128,64]{2,1,0,3:T(4,128)S(1)}, f32[8,4,16,64]{3,2,1,0:T(8,128)S(1)}, f32[8,16,64]{2,1,0:T(8,128)}, f32[8,4,16,64]{3,2,1,0:T...) while((s32[]{:T(128)}, f32[8,4,128,64]{2,1,0,3:T(4,128)S(1)}, ...), condition=%wide.region_12.13_spmd.clone, body=%wide.region_11.12_spmd.clone.sunk | while | flops 820528128 | bytes 18125500 | solution.py:109
  126.0 1.2 fusion.86
  129.3 3.5 fusion.87
  137.4 1.2 fusion.86
  140.6 3.5 fusion.87
  148.7 1.2 fusion.86
  152.0 3.5 fusion.87
  163.3 3.5 fusion.87
  171.4 1.2 fusion.86
  174.6 3.5 fusion.87
  182.7 1.2 fusion.86
  186.0 3.5 fusion.87
  194.0 1.2 fusion.86
  197.3 3.5 fusion.87
  208.6 3.5 fusion.87
  213.2 1.4 broadcast.280.clone2
  215.4 52.8 %while.31 = (s32[]{:T(128)}, f32[8,4,128,64]{2,1,0,3:T(4,128)}, f32[8,4,16,64]{3,2,1,0:T(8,128)}, s32[8,4,128]{2,1,0:T(4,128)S(1)}, f32[8,4,128,64]{2,1,0,3:T(4,...) while((s32[]{:T(128)}, f32[8,4,128,64]{2,1,0,3:T(4,128)}, ...), condition=%wide.region_5.6_spmd.clone, body=%wide.region_4.5_spmd.clone.sunk | while | flops 807780352 | bytes 14388493 | solution.py:109
  268.1 1.3 slice_multiply_fusion.5
  274.5 2.0 fusion.28
  277.2 2.6 rev.15
  279.7 2.1 copy.224
  281.9 3.4 fusion.30
  285.4 2.1 fusion.45
  288.0 1.6 multiply_reduce_fusion.8
  289.7 1.6 reduce.27
  291.4 1.5 copy.349
  293.0 1.5 reshape.471
  294.5 8.6 %all-to-all-start.1 = ((bf16[32,2,4096]{2,1,0:T(2,128)(2,1)}), bf16[32,2,4096]{2,1,0:T(2,128)(2,1)}, u32[]{:S(2)}, u32[]{:S(2)}) async-start(bf16[32,2,4096]{2,1,0:T(2,128)(2,1)} %reshape.471), calls=%async_computation.1 | async-start | bytes 1048576 | tf_op jit(solution)/shard_map/all_to_all | solution.py:198
  303.2 1.3 fusion.49
  304.6 2.8 copy.238
  307.5 2.3 reshape.469
  309.8 14.4 %all-reduce.23 = (f32[16,64]{1,0:T(8,128)S(1)}, f32[64]{0:T(128)S(1)}) all-reduce(f32[16,64]{1,0:T(8,128)S(1)} %add.336, f32[64]{0:T(128)S(1)} %copy-done.70), channel_id=1, replica_groups=mesh['dp'=8,'ctx'=32] {'dp'}, use_global_device_ids=true, to_apply=%region_26.27 | all-reduce | flops 1088 | bytes 8704 | tf_op jit(solution)/shard_map/psum | solution.py:216
  325.3 9.2 %all-to-all-start.3 = ((bf16[32,2,8192]{2,1,0:T(2,128)(2,1)}), bf16[32,2,8192]{2,1,0:T(2,128)(2,1)S(1)}, u32[]{:S(2)}, u32[]{:S(2)}) async-start(bf16[32,2,8192]{2,1,0:T(2,128)(2,1)} %reshape.469), calls=%async_computation.3 | async-start | bytes 2097152 | tf_op jit(solution)/shard_map/all_to_all | solution.py:199
  334.6 4.1 reshape.472
  338.8 3.6 copy.226
  345.2 2.9 multiply_reduce_fusion.10
  348.5 1.3 collective-permute-start
  351.0 6.3 %collective-permute-done = f32[2,2048]{1,0:T(2,128)S(1)} collective-permute-done((f32[2,2048]{1,0:T(2,128)S(1)}, f32[2,2048]{1,0:T(2,128)S(1)}, u32[]{:S(2)}, u32[]{:S(2)}) %collective-permute-start) | collective-permute-done | bytes 16416 | tf_op jit(solution)/shard_map/ppermute | solution.py:13
  357.7 2.8 fusion.39
  360.5 233.8 %all-reduce.26.cloned.1.call-done = f32[3,6144]{1,0:T(4,128)} async-done(((f32[3,6144]{1,0:T(4,128)}), f32[3,6144]{1,0:T(4,128)}) %all-reduce.26.cloned.1.call-update) | async-done | bytes 73744 | tf_op jit(solution)/shard_map/psum | solution.py:215
  594.3 1.6 broadcast_multiply_fusion.4
  595.8 1.3 reshape.470
  597.2 2.8 copy.273
  601.2 1.6 copy.244
  (625 shorter events, 132.0 us)
Async XLA Ops:
  9.1 55.8 %copy-start.2 = (bf16[1,128,6144]{1,2,0:T(8,128)(2,1)}, bf16[1,128,6144]{1,2,0:T(8,128)(2,1)S(1)}, u32[]{:S(2)}) copy-start(bf16[1,128,6144]{1,2,0:T(8,128)(2,1)S(1)} %copy.214) | copy-start | bytes 4718596
  9.1 6.5 %copy-start.72 = (s32[1,8]{1,0:T(1,128)S(1)}, s32[1,8]{1,0:T(1,128)}, u32[]{:S(2)}) copy-start(s32[1,8]{1,0:T(1,128)} %param.15) | copy-start | bytes 100
  9.1 6.7 %copy-start.33 = (f32[3,6144]{1,0:T(4,128)S(1)}, f32[3,6144]{1,0:T(4,128)}, u32[]{:S(2)}) copy-start(f32[3,6144]{1,0:T(4,128)} %param.16) | copy-start | bytes 221188
  10.4 15.3 %collective-permute-start.1 = (bf16[2,2048]{0,1:T(8,128)(2,1)}, bf16[2,2048]{0,1:T(8,128)(2,1)}, u32[]{:S(2)}, u32[]{:S(2)}) collective-permute-start(bf16[2,2048]{0,1:T(8,128)(2,1)} %slice.487), channel_id=1, source_target_pairs={{0,1},{1,2},{2,3},{3,4},{4,5},{5,6},{6,7},{7,8},{8,9},{9,10},{10,1... | collective-permute-start | bytes 24584 | tf_op jit(solution)/shard_map/ppermute | solution.py:13
  15.6 13.1 %copy-start.9 = (f32[128,2048]{0,1:T(8,128)}, f32[128,2048]{0,1:T(8,128)S(1)}, u32[]{:S(2)}) copy-start(f32[128,2048]{0,1:T(8,128)S(1)} %slice_convert_fusion) | copy-start | bytes 3145732
  15.9 12.8 %copy-start.38 = (f32[1,2048]{1,0:T(1,128)}, f32[1,2048]{1,0:T(1,128)S(1)}, u32[]{:S(2)}) copy-start(f32[1,2048]{1,0:T(1,128)S(1)} %get-tuple-element.452) | copy-start | bytes 24580
  15.9 12.8 %copy-start.40 = (f32[1,2048]{1,0:T(1,128)}, f32[1,2048]{1,0:T(1,128)S(1)}, u32[]{:S(2)}) copy-start(f32[1,2048]{1,0:T(1,128)S(1)} %get-tuple-element.453) | copy-start | bytes 24580
  15.9 12.8 %copy-start.42 = (f32[1,2048]{1,0:T(1,128)}, f32[1,2048]{1,0:T(1,128)S(1)}, u32[]{:S(2)}) copy-start(f32[1,2048]{1,0:T(1,128)S(1)} %get-tuple-element.454) | copy-start | bytes 24580
  16.6 12.1 %copy-start.50 = (f32[128]{0:T(128)}, f32[128]{0:T(128)S(1)}, u32[]{:S(2)}) copy-start(f32[128]{0:T(128)S(1)} %get-tuple-element.477) | copy-start | bytes 1540
  16.6 12.1 %copy-start.52 = (f32[128]{0:T(128)}, f32[128]{0:T(128)S(1)}, u32[]{:S(2)}) copy-start(f32[128]{0:T(128)S(1)} %get-tuple-element.478) | copy-start | bytes 1540
  17.9 10.8 %copy-start.13 = (bf16[1,128,2048]{1,2,0:T(8,128)(2,1)}, bf16[1,128,2048]{1,2,0:T(8,128)(2,1)S(1)}, u32[]{:S(2)}) copy-start(bf16[1,128,2048]{1,2,0:T(8,128)(2,1)S(1)} %copy.213) | copy-start | bytes 1572868
  26.7 11.0 %copy-start.11 = (f32[2,2048]{0,1:T(8,128)}, f32[2,2048]{0,1:T(8,128)S(1)}, u32[]{:S(2)}) copy-start(f32[2,2048]{0,1:T(8,128)S(1)} %convert_element_type.237) | copy-start | bytes 49156
  51.7 26.0 %all-to-all-start.2 = ((bf16[32,2,4096]{2,1,0:T(2,128)(2,1)}), bf16[32,2,4096]{2,1,0:T(2,128)(2,1)S(1)}, u32[]{:S(2)}, u32[]{:S(2)}) async-start(bf16[32,2,4096]{2,1,0:T(2,128)(2,1)} %reshape.467), calls=%async_computation.2 | async-start | bytes 1048576 | tf_op jit(solution)/shard_map/all_to_all | solution.py:166
  64.9 10.0 %copy-start.49 = (f32[16,64]{1,0:T(8,128)S(1)}, f32[16,64]{1,0:T(8,128)}, u32[]{:S(2)}) copy-start(f32[16,64]{1,0:T(8,128)} %param.18) | copy-start | bytes 12292
  77.7 33.2 %all-to-all-start = ((bf16[128,2,2048]{0,1,2:T(2,128)(2,1)}), bf16[128,2,2048]{0,1,2:T(2,128)(2,1)S(1)}, u32[]{:S(2)}, u32[]{:S(2)}) async-start(bf16[128,2,2048]{0,1,2:T(2,128)(2,1)} %copy.215), calls=%async_computation | async-start | bytes 2097152 | tf_op jit(solution)/shard_map/all_to_all | solution.py:165
  86.4 25.9 %copy-start.54 = (f32[64]{0:T(128)}, f32[64]{0:T(128)S(1)}, u32[]{:S(2)}) copy-start(f32[64]{0:T(128)S(1)} %get-tuple-element.446) | copy-start | bytes 772
  86.4 25.9 %copy-start.56 = (f32[64]{0:T(128)}, f32[64]{0:T(128)S(1)}, u32[]{:S(2)}) copy-start(f32[64]{0:T(128)S(1)} %get-tuple-element.447) | copy-start | bytes 772
  86.4 25.9 %copy-start.58 = (f32[64]{0:T(128)}, f32[64]{0:T(128)S(1)}, u32[]{:S(2)}) copy-start(f32[64]{0:T(128)S(1)} %get-tuple-element.448) | copy-start | bytes 772
  86.4 25.9 %copy-start.60 = (f32[64]{0:T(128)}, f32[64]{0:T(128)S(1)}, u32[]{:S(2)}) copy-start(f32[64]{0:T(128)S(1)} %get-tuple-element.449) | copy-start | bytes 772
  86.4 25.8 %copy-start.62 = (f32[64]{0:T(128)}, f32[64]{0:T(128)S(1)}, u32[]{:S(2)}) copy-start(f32[64]{0:T(128)S(1)} %get-tuple-element.450) | copy-start | bytes 772
  86.4 25.8 %copy-start.64 = (f32[64]{0:T(128)}, f32[64]{0:T(128)S(1)}, u32[]{:S(2)}) copy-start(f32[64]{0:T(128)S(1)} %get-tuple-element.451) | copy-start | bytes 772
  89.0 23.3 %copy-start.34 = (f32[4096]{0:T(1024)}, f32[4096]{0:T(1024)S(1)}, u32[]{:S(2)}) copy-start(f32[4096]{0:T(1024)S(1)} %get-tuple-element.468) | copy-start | bytes 49156
  89.0 23.3 %copy-start.36 = (f32[4096]{0:T(1024)}, f32[4096]{0:T(1024)S(1)}, u32[]{:S(2)}) copy-start(f32[4096]{0:T(1024)S(1)} %get-tuple-element.469) | copy-start | bytes 49156
  111.5 4.4 copy-start.3
  111.5 4.4 copy-start.5
  115.9 4.4 copy-start
  213.1 2.2 copy-start.17
  213.1 2.2 copy-start.19
  213.1 2.2 copy-start.25
  219.5 2.5 copy-start.24
  226.1 2.5 copy-start.24
  232.7 2.5 copy-start.24
  239.2 2.5 copy-start.24
  245.8 2.5 copy-start.24
  252.4 2.5 copy-start.24
  259.0 2.5 copy-start.24
  265.6 2.5 copy-start.24
  268.1 2.4 copy-start.22
  276.5 5.3 copy-start.46
  279.7 5.6 copy-start.1
  279.7 5.6 copy-start.71
  281.9 5.6 copy-start.35
  281.9 5.6 copy-start.37
  285.4 2.6 copy-start.16
  291.4 11.7 %copy-start.44 = (f32[4096]{0:T(1024)S(1)}, f32[4096]{0:T(1024)}, u32[]{:S(2)}) copy-start(f32[4096]{0:T(1024)} %get-tuple-element.466) | copy-start | bytes 49156
  291.4 11.7 %copy-start.45 = (f32[4096]{0:T(1024)S(1)}, f32[4096]{0:T(1024)}, u32[]{:S(2)}) copy-start(f32[4096]{0:T(1024)} %get-tuple-element.467) | copy-start | bytes 49156
  291.4 11.7 %copy-start.55 = (f32[64]{0:T(128)S(1)}, f32[64]{0:T(128)}, u32[]{:S(2)}) copy-start(f32[64]{0:T(128)} %copy-done.54) | copy-start | bytes 772
  291.4 11.7 %copy-start.57 = (f32[64]{0:T(128)S(1)}, f32[64]{0:T(128)}, u32[]{:S(2)}) copy-start(f32[64]{0:T(128)} %copy-done.56) | copy-start | bytes 772
  291.4 11.7 %copy-start.59 = (f32[64]{0:T(128)S(1)}, f32[64]{0:T(128)}, u32[]{:S(2)}) copy-start(f32[64]{0:T(128)} %copy-done.58) | copy-start | bytes 772
  291.4 11.7 %copy-start.61 = (f32[64]{0:T(128)S(1)}, f32[64]{0:T(128)}, u32[]{:S(2)}) copy-start(f32[64]{0:T(128)} %copy-done.60) | copy-start | bytes 772
  291.4 11.7 %copy-start.63 = (f32[64]{0:T(128)S(1)}, f32[64]{0:T(128)}, u32[]{:S(2)}) copy-start(f32[64]{0:T(128)} %copy-done.62) | copy-start | bytes 772
  291.4 11.7 %copy-start.65 = (f32[64]{0:T(128)S(1)}, f32[64]{0:T(128)}, u32[]{:S(2)}) copy-start(f32[64]{0:T(128)} %copy-done.64) | copy-start | bytes 772
  294.5 30.8 %all-to-all-start.1 = ((bf16[32,2,4096]{2,1,0:T(2,128)(2,1)}), bf16[32,2,4096]{2,1,0:T(2,128)(2,1)}, u32[]{:S(2)}, u32[]{:S(2)}) async-start(bf16[32,2,4096]{2,1,0:T(2,128)(2,1)} %reshape.471), calls=%async_computation.1 | async-start | bytes 1048576 | tf_op jit(solution)/shard_map/all_to_all | solution.py:198
  307.4 2.3 copy-start.48
  307.4 2.3 copy-start.26
  307.5 2.4 copy-start.70
  325.3 270.5 %all-to-all-start.3 = ((bf16[32,2,8192]{2,1,0:T(2,128)(2,1)}), bf16[32,2,8192]{2,1,0:T(2,128)(2,1)S(1)}, u32[]{:S(2)}, u32[]{:S(2)}) async-start(bf16[32,2,8192]{2,1,0:T(2,128)(2,1)} %reshape.469), calls=%async_computation.3 | async-start | bytes 2097152 | tf_op jit(solution)/shard_map/all_to_all | solution.py:199
  334.6 259.7 %all-reduce.26.cloned.1.call-start = ((), (), s32[]{:S(2)}) async-start(), calls=%async_computation.4 | async-start | bytes 196608 | tf_op jit(solution)/shard_map/psum | solution.py:215
  348.1 9.5 %copy-start.39 = (f32[1,2048]{1,0:T(1,128)S(1)}, f32[1,2048]{1,0:T(1,128)}, u32[]{:S(2)}) copy-start(f32[1,2048]{1,0:T(1,128)} %copy-done.38) | copy-start | bytes 24580
  348.1 9.5 %copy-start.41 = (f32[1,2048]{1,0:T(1,128)S(1)}, f32[1,2048]{1,0:T(1,128)}, u32[]{:S(2)}) copy-start(f32[1,2048]{1,0:T(1,128)} %copy-done.40) | copy-start | bytes 24580
  348.2 9.5 %copy-start.43 = (f32[1,2048]{1,0:T(1,128)S(1)}, f32[1,2048]{1,0:T(1,128)}, u32[]{:S(2)}) copy-start(f32[1,2048]{1,0:T(1,128)} %copy-done.42) | copy-start | bytes 24580
  348.2 9.5 %copy-start.68 = (f32[128]{0:T(128)S(1)}, f32[128]{0:T(128)}, u32[]{:S(2)}) copy-start(f32[128]{0:T(128)} %get-tuple-element.476) | copy-start | bytes 1540
  348.2 9.5 %copy-start.69 = (f32[128]{0:T(128)S(1)}, f32[128]{0:T(128)}, u32[]{:S(2)}) copy-start(f32[128]{0:T(128)} %get-tuple-element.479) | copy-start | bytes 1540
  348.5 8.8 %collective-permute-start = (f32[2,2048]{1,0:T(2,128)S(1)}, f32[2,2048]{1,0:T(2,128)S(1)}, u32[]{:S(2)}, u32[]{:S(2)}) collective-permute-start(f32[2,2048]{1,0:T(2,128)S(1)} %copy.228), channel_id=1, source_target_pairs={{1,0},{2,1},{3,2},{4,3},{5,4},{6,5},{7,6},{8,7},{9,8},{10,9},{11,1... | collective-permute-start | bytes 49160 | tf_op jit(solution)/shard_map/ppermute | solution.py:13
  (58 other events, 95.8 us)
Sparse Core Ops, SparseCore 0:
  351.1 243.1 all-reduce.25
where the time goes:
time: 621 us; the launch traced here: 610 us
  waiting for transfers between devices  252 us (41%)
  local copies, waits for them, and re-layouts  151 us (24%)
  other arithmetic  67.8 us (11%)
  matrix products  60.7 us (10%)
  starting transfers between devices  46 us (7%)
  between operations  15.7 us (3%)
  blocking collectives  14.4 us (2%)
    psum x1, waiting for transfers between devices, per_device(): grad_taps = lax.psum(tap_sum, ('dp', 'ctx')) * grad_scale  234 us
    dot_general x8, matrix products, group_fn(): jnp.einsum('pic,pimc->mc', other_blk, inner_state, precision=lax.Precisio...  27.9 us
    unnamed x151, local copies, waits for them, and re-layouts  23.1 us
    dynamic_slice x40, local copies, waits for them, and re-layouts, modal_sweep(): lax.map(group_fn, (src_groups, seg_groups, other_groups))  22.3 us
    dot_general x16, matrix products, group_fn(): jnp.einsum('pij,pjk->pik', joined_mask, lifted, precision=lax.Precision.H...  19.2 us
    slice x16, local copies, waits for them, and re-layouts, group_fn(): last_row = inner_state[:, -1]  18.7 us
    dynamic_update_slice x64, local copies, waits for them, and re-layouts, modal_sweep(): lax.map(group_fn, (src_groups, seg_groups, other_groups))  18.4 us
    psum x1, blocking collectives, per_device(): resid_sum, skip_sum = lax.psum((grad_resid, skip_part), 'dp')  14.4 us
  transfers between devices with their start and end apart: 7, of which 5 were waited for; matrix products, arithmetic and copies ran while one was open for 10% of the time, Pallas kernels for 0%

commit v1 on v0

--- a/solution.py
+++ b/solution.py
@@ -212,7 +212,7 @@
     )
     placed = lax.dynamic_update_slice(placed, kv_taps, (0, 1, shard_index * per_shard))
     tap_sum = placed.reshape(3, 3 * channels)
-    grad_taps = lax.psum(tap_sum, ("dp", "ctx")) * grad_scale
+    grad_taps = lax.psum(lax.psum(tap_sum, "dp"), "ctx") * grad_scale
     resid_sum, skip_sum = lax.psum((grad_resid, skip_part), "dp")
     return (grad_feats[None], grad_taps, resid_sum * grad_scale, skip_sum * grad_scale)
 

time: 621 us -> 586 us (0.944)
  the two profiles are of different devices: /device:TPU:1 before, /device:TPU:2 now
where the time goes in v1:
time: 586 us; the launch traced here: 575 us
  waiting for transfers between devices  222 us (38%)
  local copies, waits for them, and re-layouts  153 us (26%)
  other arithmetic  70.9 us (12%)
  matrix products  60.7 us (10%)
  starting transfers between devices  39 us (7%)
  between operations  15.7 us (3%)
  blocking collectives  11.3 us (2%)
    psum x2, waiting for transfers between devices, per_device(): grad_taps = lax.psum(lax.psum(tap_sum, 'dp'), 'ctx') * grad_scale  195 us
    dot_general x8, matrix products, group_fn(): jnp.einsum('pic,pimc->mc', other_blk, inner_state, precision=lax.Precisio...  27.9 us
    unnamed x145, local copies, waits for them, and re-layouts  25.1 us
    dynamic_slice x40, local copies, waits for them, and re-layouts, modal_sweep(): lax.map(group_fn, (src_groups, seg_groups, other_groups))  22.3 us
    dot_general x16, matrix products, group_fn(): jnp.einsum('pij,pjk->pik', joined_mask, lifted, precision=lax.Precision.H...  19.2 us
    slice x16, local copies, waits for them, and re-layouts, group_fn(): last_row = inner_state[:, -1]  18.7 us
    dynamic_update_slice x64, local copies, waits for them, and re-layouts, modal_sweep(): lax.map(group_fn, (src_groups, seg_groups, other_groups))  18.4 us
    ppermute x2, waiting for transfers between devices, from_behind(): return lax.ppermute(block, axis, route)  16.3 us
  transfers between devices with their start and end apart: 8, of which 6 were waited for; matrix products, arithmetic and copies ran while one was open for 11% of the time, Pallas kernels for 0%

profile of v1, /device:TPU:2, one launch (start us, length us, event | category | flops | bytes accessed | tf_op | source)
XLA Modules:
  0.0 574.7 jit_solution(10711756989787082222)
XLA Ops:
  7.2 1.9 copy.214
  9.1 1.2 slice.487
  10.4 4.6 collective-permute-start.1
  16.0 1.3 copy.213
  17.4 8.3 %collective-permute-done.1 = bf16[2,2048]{0,1:T(8,128)(2,1)} collective-permute-done((bf16[2,2048]{0,1:T(8,128)(2,1)}, bf16[2,2048]{0,1:T(8,128)(2,1)}, u32[]{:S(2)}, u32[]{:S(2)}) %collective-permute-start.1) | collective-permute-done | bytes 8224 | tf_op jit(solution)/shard_map/ppermute | solution.py:13
  26.8 1.9 fusion.46
  28.8 8.9 %copy.348 = bf16[128,1,2048]{0,1,2:T(2,128)(2,1)} copy(bf16[128,1,2048]{0,2,1:T(8,128)(2,1)S(1)} %fusion.46) | data formatting | bytes 1048576 | tf_op jit(solution)/shard_map/broadcast_in_dim | solution.py:164
  38.3 12.5 %reduce.26 = bf16[2048,128]{1,0:T(8,128)(2,1)S(1)} reduce(bf16[2048,1,128]{2,1,0:T(2,128)(2,1)} %bitcast.298, bf16[]{:T(256)} %broadcast.332), dimensions={1}, to_apply=%bitcast.221.reduce_sub_computation | reduce | bytes 1048578
  51.8 13.4 %all-to-all-start.2 = ((bf16[32,2,4096]{2,1,0:T(2,128)(2,1)}), bf16[32,2,4096]{2,1,0:T(2,128)(2,1)S(1)}, u32[]{:S(2)}, u32[]{:S(2)}) async-start(bf16[32,2,4096]{2,1,0:T(2,128)(2,1)} %reshape.467), calls=%async_computation.2 | async-start | bytes 1048576 | tf_op jit(solution)/shard_map/all_to_all | solution.py:166
  65.4 9.5 %copy.215 = bf16[128,2,2048]{0,1,2:T(2,128)(2,1)} copy(bf16[128,2,2048]{0,2,1:T(8,128)(2,1)S(1)} %bitcast.297) | data formatting | bytes 2097152 | tf_op jit(solution)/shard_map/reshape | solution.py:163
  76.6 5.0 all-to-all-done.2
  81.6 5.2 all-to-all-start
  91.8 1.6 copy.346
  93.4 13.4 %rev.13 = f32[4096,64]{0,1:T(8,128)S(1)} reverse(f32[4096,64]{0,1:T(8,128)} %bitcast.302), dimensions={0} | reverse | bytes 2097152 | tf_op jit(solution)/shard_map/rev | solution.py:180
  106.8 1.7 reshape.428
  108.5 6.1 %all-to-all-done = bf16[128,2,2048]{0,1,2:T(2,128)(2,1)S(1)} async-done(((bf16[128,2,2048]{0,1,2:T(2,128)(2,1)}), bf16[128,2,2048]{0,1,2:T(2,128)(2,1)S(1)}, u32[]{:S(2)}, u32[]{:S(2)}) %all-to-all-start) | async-done | bytes 1048608 | tf_op jit(solution)/shard_map/all_to_all | solution.py:165
  116.1 3.6 multiply_reduce_fusion.2
  119.7 2.6 rev.14
  122.3 1.8 reshape.422
  124.1 1.7 reshape.429
  126.1 90.9 %while.32 = (s32[]{:T(128)}, f32[8,4,128,64]{2,1,0,3:T(4,128)S(1)}, f32[8,4,16,64]{3,2,1,0:T(8,128)S(1)}, f32[8,16,64]{2,1,0:T(8,128)}, f32[8,4,16,64]{3,2,1,0:T...) while((s32[]{:T(128)}, f32[8,4,128,64]{2,1,0,3:T(4,128)S(1)}, ...), condition=%wide.region_12.13_spmd.clone, body=%wide.region_11.12_spmd.clone.sunk | while | flops 820528128 | bytes 18125500 | solution.py:109
  129.9 1.2 fusion.86
  133.1 3.5 fusion.87
  141.2 1.2 fusion.86
  144.5 3.5 fusion.87
  155.8 3.5 fusion.87
  167.1 3.5 fusion.87
  175.2 1.2 fusion.86
  178.5 3.5 fusion.87
  189.8 3.5 fusion.87
  197.9 1.2 fusion.86
  201.1 3.5 fusion.87
  209.2 1.2 fusion.86
  212.5 3.5 fusion.87
  217.0 1.5 broadcast.280.clone2
  219.2 52.8 %while.31 = (s32[]{:T(128)}, f32[8,4,128,64]{2,1,0,3:T(4,128)}, f32[8,4,16,64]{3,2,1,0:T(8,128)}, s32[8,4,128]{2,1,0:T(4,128)S(1)}, f32[8,4,128,64]{2,1,0,3:T(4,...) while((s32[]{:T(128)}, f32[8,4,128,64]{2,1,0,3:T(4,128)}, ...), condition=%wide.region_5.6_spmd.clone, body=%wide.region_4.5_spmd.clone.sunk | while | flops 807780352 | bytes 14388493 | solution.py:109
  272.0 1.3 slice_multiply_fusion.5
  278.4 2.0 fusion.28
  281.0 2.6 rev.15
  283.6 2.2 copy.224
  285.7 3.4 fusion.30
  289.2 2.3 fusion.45
  291.5 2.7 reduce.27
  294.3 2.6 copy.349
  296.8 3.0 reshape.471
  299.8 5.2 all-to-all-start.1
  305.2 3.3 multiply_reduce_fusion.8
  308.5 1.3 fusion.49
  310.0 2.8 copy.238
  312.9 2.3 reshape.469
  315.3 11.3 %all-reduce.23 = (f32[16,64]{1,0:T(8,128)S(1)}, f32[64]{0:T(128)S(1)}) all-reduce(f32[16,64]{1,0:T(8,128)S(1)} %add.338, f32[64]{0:T(128)S(1)} %copy-done.67), channel_id=1, replica_groups=mesh['dp'=8,'ctx'=32] {'dp'}, use_global_device_ids=true, to_apply=%region_27.28 | all-reduce | flops 1088 | bytes 8704 | tf_op jit(solution)/shard_map/psum | solution.py:216
  327.2 9.2 %all-to-all-start.3 = ((bf16[32,2,8192]{2,1,0:T(2,128)(2,1)}), bf16[32,2,8192]{2,1,0:T(2,128)(2,1)S(1)}, u32[]{:S(2)}, u32[]{:S(2)}) async-start(bf16[32,2,8192]{2,1,0:T(2,128)(2,1)} %reshape.469), calls=%async_computation.3 | async-start | bytes 2097152 | tf_op jit(solution)/shard_map/all_to_all | solution.py:199
  336.5 4.1 reshape.472
  340.6 3.6 copy.226
  347.1 2.9 multiply_reduce_fusion.10
  351.6 1.3 collective-permute-start
  353.4 8.0 %collective-permute-done = f32[2,2048]{1,0:T(2,128)S(1)} collective-permute-done((f32[2,2048]{1,0:T(2,128)S(1)}, f32[2,2048]{1,0:T(2,128)S(1)}, u32[]{:S(2)}, u32[]{:S(2)}) %collective-permute-start) | collective-permute-done | bytes 16416 | tf_op jit(solution)/shard_map/ppermute | solution.py:13
  361.8 51.7 %all-reduce.27.cloned.1.call-done = f32[3,6144]{1,0:T(4,128)} async-done(((f32[3,6144]{1,0:T(4,128)}), f32[3,6144]{1,0:T(4,128)}) %all-reduce.27.cloned.1.call-update) | async-done | bytes 73744 | tf_op jit(solution)/shard_map/psum | solution.py:215
  413.5 2.8 fusion.39
  416.3 142.9 %all-reduce.29.cloned.1.call-done = f32[3,6144]{1,0:T(4,128)} async-done(((f32[3,6144]{1,0:T(4,128)}), f32[3,6144]{1,0:T(4,128)}) %all-reduce.29.cloned.1.call-update) | async-done | bytes 73744 | tf_op jit(solution)/shard_map/psum | solution.py:215
  559.3 1.6 broadcast_multiply_fusion.4
  560.8 1.3 reshape.470
  562.2 2.8 copy.273
  566.1 1.6 copy.244
  (622 shorter events, 132.8 us)
Async XLA Ops:
  9.1 56.2 %copy-start.2 = (bf16[1,128,6144]{1,2,0:T(8,128)(2,1)}, bf16[1,128,6144]{1,2,0:T(8,128)(2,1)S(1)}, u32[]{:S(2)}) copy-start(bf16[1,128,6144]{1,2,0:T(8,128)(2,1)S(1)} %copy.214) | copy-start | bytes 4718596
  9.1 6.0 %copy-start.69 = (s32[1,8]{1,0:T(1,128)S(1)}, s32[1,8]{1,0:T(1,128)}, u32[]{:S(2)}) copy-start(s32[1,8]{1,0:T(1,128)} %param.15) | copy-start | bytes 100
  9.1 6.2 %copy-start.30 = (f32[3,6144]{1,0:T(4,128)S(1)}, f32[3,6144]{1,0:T(4,128)}, u32[]{:S(2)}) copy-start(f32[3,6144]{1,0:T(4,128)} %param.16) | copy-start | bytes 221188
  10.4 15.3 %collective-permute-start.1 = (bf16[2,2048]{0,1:T(8,128)(2,1)}, bf16[2,2048]{0,1:T(8,128)(2,1)}, u32[]{:S(2)}, u32[]{:S(2)}) collective-permute-start(bf16[2,2048]{0,1:T(8,128)(2,1)} %slice.487), channel_id=1, source_target_pairs={{0,1},{1,2},{2,3},{3,4},{4,5},{5,6},{6,7},{7,8},{8,9},{9,10},{10,1... | collective-permute-start | bytes 24584 | tf_op jit(solution)/shard_map/ppermute | solution.py:13
  15.1 13.7 %copy-start.9 = (f32[128,2048]{0,1:T(8,128)}, f32[128,2048]{0,1:T(8,128)S(1)}, u32[]{:S(2)}) copy-start(f32[128,2048]{0,1:T(8,128)S(1)} %slice_convert_fusion) | copy-start | bytes 3145732
  15.3 13.4 %copy-start.35 = (f32[1,2048]{1,0:T(1,128)}, f32[1,2048]{1,0:T(1,128)S(1)}, u32[]{:S(2)}) copy-start(f32[1,2048]{1,0:T(1,128)S(1)} %get-tuple-element.452) | copy-start | bytes 24580
  15.3 13.4 %copy-start.37 = (f32[1,2048]{1,0:T(1,128)}, f32[1,2048]{1,0:T(1,128)S(1)}, u32[]{:S(2)}) copy-start(f32[1,2048]{1,0:T(1,128)S(1)} %get-tuple-element.453) | copy-start | bytes 24580
  15.3 13.4 %copy-start.39 = (f32[1,2048]{1,0:T(1,128)}, f32[1,2048]{1,0:T(1,128)S(1)}, u32[]{:S(2)}) copy-start(f32[1,2048]{1,0:T(1,128)S(1)} %get-tuple-element.454) | copy-start | bytes 24580
  16.0 12.7 %copy-start.47 = (f32[128]{0:T(128)}, f32[128]{0:T(128)S(1)}, u32[]{:S(2)}) copy-start(f32[128]{0:T(128)S(1)} %get-tuple-element.477) | copy-start | bytes 1540
  16.0 12.7 %copy-start.49 = (f32[128]{0:T(128)}, f32[128]{0:T(128)S(1)}, u32[]{:S(2)}) copy-start(f32[128]{0:T(128)S(1)} %get-tuple-element.478) | copy-start | bytes 1540
  17.3 11.4 %copy-start.13 = (bf16[1,128,2048]{1,2,0:T(8,128)(2,1)}, bf16[1,128,2048]{1,2,0:T(8,128)(2,1)S(1)}, u32[]{:S(2)}) copy-start(bf16[1,128,2048]{1,2,0:T(8,128)(2,1)S(1)} %copy.213) | copy-start | bytes 1572868
  26.8 11.0 %copy-start.11 = (f32[2,2048]{0,1:T(8,128)}, f32[2,2048]{0,1:T(8,128)S(1)}, u32[]{:S(2)}) copy-start(f32[2,2048]{0,1:T(8,128)S(1)} %convert_element_type.237) | copy-start | bytes 49156
  51.8 29.9 %all-to-all-start.2 = ((bf16[32,2,4096]{2,1,0:T(2,128)(2,1)}), bf16[32,2,4096]{2,1,0:T(2,128)(2,1)S(1)}, u32[]{:S(2)}, u32[]{:S(2)}) async-start(bf16[32,2,4096]{2,1,0:T(2,128)(2,1)} %reshape.467), calls=%async_computation.2 | async-start | bytes 1048576 | tf_op jit(solution)/shard_map/all_to_all | solution.py:166
  65.3 10.0 %copy-start.46 = (f32[16,64]{1,0:T(8,128)S(1)}, f32[16,64]{1,0:T(8,128)}, u32[]{:S(2)}) copy-start(f32[16,64]{1,0:T(8,128)} %param.18) | copy-start | bytes 12292
  81.6 33.0 %all-to-all-start = ((bf16[128,2,2048]{0,1,2:T(2,128)(2,1)}), bf16[128,2,2048]{0,1,2:T(2,128)(2,1)S(1)}, u32[]{:S(2)}, u32[]{:S(2)}) async-start(bf16[128,2,2048]{0,1,2:T(2,128)(2,1)} %copy.215), calls=%async_computation | async-start | bytes 2097152 | tf_op jit(solution)/shard_map/all_to_all | solution.py:165
  86.9 29.1 %copy-start.51 = (f32[64]{0:T(128)}, f32[64]{0:T(128)S(1)}, u32[]{:S(2)}) copy-start(f32[64]{0:T(128)S(1)} %get-tuple-element.446) | copy-start | bytes 772
  86.9 29.1 %copy-start.53 = (f32[64]{0:T(128)}, f32[64]{0:T(128)S(1)}, u32[]{:S(2)}) copy-start(f32[64]{0:T(128)S(1)} %get-tuple-element.447) | copy-start | bytes 772
  86.9 29.1 %copy-start.55 = (f32[64]{0:T(128)}, f32[64]{0:T(128)S(1)}, u32[]{:S(2)}) copy-start(f32[64]{0:T(128)S(1)} %get-tuple-element.448) | copy-start | bytes 772
  86.9 29.1 %copy-start.57 = (f32[64]{0:T(128)}, f32[64]{0:T(128)S(1)}, u32[]{:S(2)}) copy-start(f32[64]{0:T(128)S(1)} %get-tuple-element.449) | copy-start | bytes 772
  86.9 29.1 %copy-start.59 = (f32[64]{0:T(128)}, f32[64]{0:T(128)S(1)}, u32[]{:S(2)}) copy-start(f32[64]{0:T(128)S(1)} %get-tuple-element.450) | copy-start | bytes 772
  86.9 29.1 %copy-start.61 = (f32[64]{0:T(128)}, f32[64]{0:T(128)S(1)}, u32[]{:S(2)}) copy-start(f32[64]{0:T(128)S(1)} %get-tuple-element.451) | copy-start | bytes 772
  89.5 26.5 %copy-start.31 = (f32[4096]{0:T(1024)}, f32[4096]{0:T(1024)S(1)}, u32[]{:S(2)}) copy-start(f32[4096]{0:T(1024)S(1)} %get-tuple-element.468) | copy-start | bytes 49156
  89.5 26.6 %copy-start.33 = (f32[4096]{0:T(1024)}, f32[4096]{0:T(1024)S(1)}, u32[]{:S(2)}) copy-start(f32[4096]{0:T(1024)S(1)} %get-tuple-element.469) | copy-start | bytes 49156
  115.2 4.5 copy-start.3
  115.2 4.5 copy-start.5
  119.7 4.4 copy-start
  223.3 2.5 copy-start.21
  229.9 2.5 copy-start.21
  236.5 2.5 copy-start.21
  243.1 2.5 copy-start.21
  249.7 2.5 copy-start.21
  256.2 2.5 copy-start.21
  262.8 2.5 copy-start.21
  269.4 2.5 copy-start.21
  272.0 2.4 copy-start.19
  280.4 5.4 copy-start.43
  283.6 5.6 copy-start.1
  283.6 5.6 copy-start.68
  294.3 10.8 %copy-start.4 = (f32[4096,64]{0,1:T(8,128)S(1)}, f32[4096,64]{0,1:T(8,128)}, u32[]{:S(2)}) copy-start(f32[4096,64]{0,1:T(8,128)} %copy-done.3) | copy-start | bytes 3145732
  294.3 10.8 %copy-start.6 = (f32[4096,64]{0,1:T(8,128)S(1)}, f32[4096,64]{0,1:T(8,128)}, u32[]{:S(2)}) copy-start(f32[4096,64]{0,1:T(8,128)} %copy-done.5) | copy-start | bytes 3145732
  294.3 10.8 %copy-start.8 = (bf16[2,32,8,8,128]{4,3,1,2,0:T(8,128)(2,1)S(1)}, bf16[2,32,8,8,128]{4,3,1,2,0:T(8,128)(2,1)}, u32[]{:S(2)}) copy-start(bf16[2,32,8,8,128]{4,3,1,2,0:T(8,128)(2,1)} %copy-done.7) | copy-start | bytes 3145732
  294.3 10.8 %copy-start.32 = (f32[4096]{0:T(1024)S(1)}, f32[4096]{0:T(1024)}, u32[]{:S(2)}) copy-start(f32[4096]{0:T(1024)} %copy-done.31) | copy-start | bytes 49156
  294.3 10.8 %copy-start.34 = (f32[4096]{0:T(1024)S(1)}, f32[4096]{0:T(1024)}, u32[]{:S(2)}) copy-start(f32[4096]{0:T(1024)} %copy-done.33) | copy-start | bytes 49156
  299.8 27.4 %all-to-all-start.1 = ((bf16[32,2,4096]{2,1,0:T(2,128)(2,1)}), bf16[32,2,4096]{2,1,0:T(2,128)(2,1)}, u32[]{:S(2)}, u32[]{:S(2)}) async-start(bf16[32,2,4096]{2,1,0:T(2,128)(2,1)} %reshape.471), calls=%async_computation.1 | async-start | bytes 1048576 | tf_op jit(solution)/shard_map/all_to_all | solution.py:198
  305.1 3.4 copy-start.41
  305.1 3.4 copy-start.42
  305.1 3.4 copy-start.52
  305.1 3.4 copy-start.54
  305.1 3.4 copy-start.56
  305.1 3.4 copy-start.58
  305.1 3.4 copy-start.60
  305.1 3.4 copy-start.62
  312.9 2.3 copy-start.45
  312.9 2.3 copy-start.23
  312.9 2.4 copy-start.67
  327.2 233.6 %all-to-all-start.3 = ((bf16[32,2,8192]{2,1,0:T(2,128)(2,1)}), bf16[32,2,8192]{2,1,0:T(2,128)(2,1)S(1)}, u32[]{:S(2)}, u32[]{:S(2)}) async-start(bf16[32,2,8192]{2,1,0:T(2,128)(2,1)} %reshape.469), calls=%async_computation.3 | async-start | bytes 2097152 | tf_op jit(solution)/shard_map/all_to_all | solution.py:199
  336.4 77.0 %all-reduce.27.cloned.1.call-start = ((), (), s32[]{:S(2)}) async-start(), calls=%async_computation.4 | async-start | bytes 196608 | tf_op jit(solution)/shard_map/psum | solution.py:215
  350.0 63.5 %copy-start.36 = (f32[1,2048]{1,0:T(1,128)S(1)}, f32[1,2048]{1,0:T(1,128)}, u32[]{:S(2)}) copy-start(f32[1,2048]{1,0:T(1,128)} %copy-done.35) | copy-start | bytes 24580
  350.0 63.5 %copy-start.38 = (f32[1,2048]{1,0:T(1,128)S(1)}, f32[1,2048]{1,0:T(1,128)}, u32[]{:S(2)}) copy-start(f32[1,2048]{1,0:T(1,128)} %copy-done.37) | copy-start | bytes 24580
  350.0 63.5 %copy-start.40 = (f32[1,2048]{1,0:T(1,128)S(1)}, f32[1,2048]{1,0:T(1,128)}, u32[]{:S(2)}) copy-start(f32[1,2048]{1,0:T(1,128)} %copy-done.39) | copy-start | bytes 24580
  350.0 63.5 %copy-start.65 = (f32[128]{0:T(128)S(1)}, f32[128]{0:T(128)}, u32[]{:S(2)}) copy-start(f32[128]{0:T(128)} %get-tuple-element.476) | copy-start | bytes 1540
  350.0 63.5 %copy-start.66 = (f32[128]{0:T(128)S(1)}, f32[128]{0:T(128)}, u32[]{:S(2)}) copy-start(f32[128]{0:T(128)} %get-tuple-element.479) | copy-start | bytes 1540
  351.2 208.0 %all-reduce.29.cloned.1.call-start = ((), (), s32[]{:S(2)}) async-start(), calls=%async_computation.5 | async-start | bytes 196608 | tf_op jit(solution)/shard_map/psum | solution.py:215
  351.6 9.8 %collective-permute-start = (f32[2,2048]{1,0:T(2,128)S(1)}, f32[2,2048]{1,0:T(2,128)S(1)}, u32[]{:S(2)}, u32[]{:S(2)}) collective-permute-start(f32[2,2048]{1,0:T(2,128)S(1)} %copy.228), channel_id=1, source_target_pairs={{1,0},{2,1},{3,2},{4,3},{5,4},{6,5},{7,6},{8,7},{9,8},{10,9},{11,1... | collective-permute-start | bytes 49160 | tf_op jit(solution)/shard_map/ppermute | solution.py:13
  (56 other events, 92.3 us)
Sparse Core Ops, SparseCore 0:
  351.4 62.0 all-reduce.26
  417.3 141.9 all-reduce.28
